TPU v7x, 32 devices: a whole 2x2x4 slice. The times are simulated.
32 devices in a mesh: row: 16 (over z, y, core), col: 2 (over x).
Axes of the slice: x: 2, y: 2, z: 4, core: 2. Of those that a mesh axis runs over, the one named last changes fastest.
Arguments:
- blocks: bfloat16 [32768, 4096], P('row', 'col'), may hold values from -0.046875 to 0.046875
- factors: float32 [64, 512, 512], P('row'), as said below
- block_live: int32 [64], P('row'), may hold values from 1 to 512, 24576 in all
Outputs:
- schur_matrix: float32 [4096, 4096], P('row', 'col')
- panel_factor: float32 [4096, 512], P('row', 'col')
Inputs may be any that keep to these rules, and one draw needn't show every extreme that they name: `factors`: each block is lower triangular with a positive diagonal and zeros above it. `block_live`: rows of a block at or beyond its count are left out.
All inputs are finite; a program needn't handle non-finite values.
Results may differ from a plain program's by a relative error of at most 0.0014.
Values may be sent and summed in bfloat16 or wider, within the bound.
No kernel may reach another device: no remote copies, remote signals or barrier semaphores. Data moves between devices by JAX's collectives and lax.ppermute only.
A program may use at most 128 MiB of HBM per device.

v0:
```python
import jax
import jax.numpy as jnp
from jax import lax
from jax.sharding import PartitionSpec as P

LEAD = 512


def from_root(value, axis, source):
    kept = jnp.where(lax.axis_index(axis) == source, value, 0).astype(value.dtype)
    return lax.psum(kept, axis)


def whiten(segment, factors, block_live):
    count_blocks = factors.shape[0]
    order = factors.shape[1]
    columns = segment.shape[1]
    shaped = segment.reshape(count_blocks, order, columns).astype(jnp.float32)
    solved = jax.vmap(
        lambda factor, right: jax.scipy.linalg.solve_triangular(factor, right, lower=True)
    )(factors, shaped)
    row_index = jnp.arange(order, dtype=jnp.int32)
    solved = jnp.where(row_index[None, :, None] < block_live[:, None, None], solved, 0.0)
    return solved.reshape(count_blocks * order, columns).astype(jnp.bfloat16)


def body(blocks, factors, block_live):
    panel_width = blocks.shape[1]
    raw_rows = lax.all_gather(blocks, "col", axis=1, tiled=True)
    gathered = whiten(raw_rows, factors, block_live)
    own_panel = lax.dynamic_slice_in_dim(
        gathered, lax.axis_index("col") * panel_width, panel_width, 1
    )
    all_columns = gathered.shape[1]
    slab_rows = all_columns // lax.axis_size("row")
    schur_slab = lax.psum_scatter(
        lax.dot_general(
            gathered, own_panel, (((0,), (0,)), ((), ())), preferred_element_type=jnp.float32
        ),
        "row",
        scatter_dimension=0,
        tiled=True,
    )
    leading_here = schur_slab[:, :LEAD]
    leading_cols = from_root(leading_here, "col", 0)
    pieces = []
    for source in range(LEAD // slab_rows):
        pieces.append(from_root(leading_cols, "row", source))
    leading_block = jnp.concatenate(pieces, axis=0)
    lead_factor = jnp.linalg.cholesky(leading_block)
    lead_inverse = jax.scipy.linalg.solve_triangular(
        lead_factor, jnp.eye(LEAD, dtype=jnp.float32), lower=True
    )
    out_width = LEAD // lax.axis_size("col")
    inverse_rows = lax.dynamic_slice_in_dim(
        lead_inverse, lax.axis_index("col") * out_width, out_width, 0
    )
    panel_factor = jnp.dot(leading_cols, inverse_rows.T, precision=lax.Precision.HIGHEST)
    return (schur_slab, panel_factor)


def solution(mesh):
    in_specs = (P("row", "col"), P("row", None, None), P("row"))
    out_specs = (P("row", "col"), P("row", "col"))
    return jax.shard_map(body, mesh=mesh, in_specs=in_specs, out_specs=out_specs, check_vma=False)
```

profile of v0, /device:TPU:0, one launch (start us, length us, event | category | flops | bytes accessed | tf_op | source)
XLA Modules:
  0.0 1007.4 jit_solution(10435521122537996568)
XLA Ops:
  7.2 0.7 all-gather.2.cloned.1.call-update
  8.1 4.8 broadcast_select_fusion
  12.8 13.0 %while.2 = (s32[]{:T(128)}, f32[4,512,512]{2,1,0:T(8,128)}, s32[4,2]{0,1:T(2,128)S(1)}, f32[4,4,128,128]{3,2,0,1:T(8,128)S(1)}, s32[]{:T(128)}) while((s32[]{:T(128)}, f32[4,512,512]{2,1,0:T(8,128)}, s32[4,2]{0,1:T(2,128)S(1)}, f32[4,4,128,128]{3,2,0,1:T(8,128)S(1)}, s32[]{:T(128)}) %tuple.47), condition=%wide.while_cond, body=%wide.while_body.sunk | while | flops 2 | bytes 524397 | solution.py:20
  13.5 2.5 bitcast_dynamic-update-slice_fusion.4
  16.6 2.6 bitcast_dynamic-update-slice_fusion.4
  19.9 2.7 bitcast_dynamic-update-slice_fusion.4
  23.3 2.5 bitcast_dynamic-update-slice_fusion.4
  26.4 157.2 %custom-call.35 = f32[4,4,128,128]{2,3,1,0:T(8,128)S(1)} custom-call(f32[4,4,128,128]{3,2,1,0:T(8,128)S(1)} %bitcast.87), custom_call_target="InvertDiagBlocksLowerTriangular" | custom-call | tf_op jit(solution)/shard_map/vmap(jit(_solve_triangular))/triangular_solve | solution.py:20
  183.7 27.5 %all-gather.2.cloned.1.call-done = bf16[2048,4096]{1,0:T(8,128)(2,1)} async-done(((bf16[2048,2048]{1,0:T(8,128)(2,1)}), bf16[2048,4096]{1,0:T(8,128)(2,1)}) %all-gather.2.cloned.1.call-update) | async-done | bytes 16777232 | tf_op jit(solution)/shard_map/all_gather | solution.py:29
  211.2 18.6 %convert_element_type.17 = f32[4,512,4096]{2,1,0:T(8,128)} convert(bf16[4,512,4096]{2,1,0:T(8,128)(2,1)} %bitcast.84) | non-fusion elementwise | flops 8388608 | bytes 50331648 | tf_op jit(solution)/shard_map/convert_element_type | solution.py:18
  229.8 5.8 fusion.16
  235.7 8.8 fusion.36
  244.4 11.6 %fusion.13 = f32[4,128,4096]{2,1,0:T(8,128)} fusion(f32[4,128,4096]{2,1,0:T(8,128)S(1)} %fusion.36, f32[4,512,4096]{2,1,0:T(8,128)} %convert_element_type.17, f32[4,4,128,128]{2,3,1,0:T(8,128)S(1)} %custom-call.35), kind=kOutput, calls=%fused_computation.22 | convolution fusion | flops 3223322624 | bytes 25427968 | tf_op jit(solution)/shard_map/vmap(jit(_solve_triangular))/triangular_solve | solution.py:20
  256.1 14.1 %fusion.7 = f32[4,128,4096]{2,1,0:T(8,128)} fusion(f32[4,128,4096]{2,1,0:T(8,128)} %fusion.13, f32[4,128,4096]{2,1,0:T(8,128)S(1)} %fusion.16, f32[4,512,512]{2,1,0:T(8,128)} %get-tuple-element.156), kind=kOutput, calls=%fused_computation.13 | convolution fusion | flops 6446645248 | bytes 25690112 | tf_op jit(solution)/shard_map/vmap(jit(_solve_triangular))/triangular_solve | solution.py:20
  270.2 12.9 %fusion.12 = f32[4,128,4096]{2,1,0:T(8,128)} fusion(f32[4,128,4096]{2,1,0:T(8,128)} %fusion.7, f32[4,512,4096]{2,1,0:T(8,128)} %convert_element_type.17, f32[4,4,128,128]{2,3,1,0:T(8,128)S(1)} %custom-call.35), kind=kOutput, calls=%fused_computation.20 | convolution fusion | flops 3223322624 | bytes 25427968 | tf_op jit(solution)/shard_map/vmap(jit(_solve_triangular))/triangular_solve | solution.py:20
  283.1 23.1 %fusion.1 = f32[4,128,4096]{2,1,0:T(8,128)} fusion(f32[4,128,4096]{2,1,0:T(8,128)} %fusion.12, f32[4,128,4096]{2,1,0:T(8,128)} %fusion.13, f32[4,128,4096]{2,1,0:T(8,128)} %copy-done, f32[4,512,512]{2,1,0:T(8,128)} %get-tuple-element.156), kind=kOutput, calls=%fused_computation.7 | convolution fusion | flops 9676259328 | bytes 34340864 | tf_op jit(solution)/shard_map/vmap(jit(_solve_triangular))/triangular_solve | solution.py:20
  306.2 12.5 %fusion.11 = bf16[4,128,4096]{2,1,0:T(8,128)(2,1)} fusion(f32[4,128,4096]{2,1,0:T(8,128)} %fusion.1, f32[4,512,4096]{2,1,0:T(8,128)} %convert_element_type.17, f32[4,4,128,128]{2,3,1,0:T(8,128)S(1)} %custom-call.35), kind=kOutput, calls=%fused_computation.18 | convolution fusion | flops 3223322624 | bytes 21233664 | tf_op jit(solution)/shard_map/vmap(jit(_solve_triangular))/triangular_solve | solution.py:20
  318.7 16.8 %pad_maximum_fusion = bf16[4,512,4096]{2,1,0:T(8,128)(2,1)} fusion(bf16[4,128,4096]{2,1,0:T(8,128)(2,1)} %fusion.11, f32[4,128,4096]{2,1,0:T(8,128)} %fusion.12, f32[4,128,4096]{2,1,0:T(8,128)} %fusion.13, f32[4,128,4096]{2,1,0:T(8,128)} %copy-done), kind=kLoop, calls=%fused_computation.4 | loop fusion | flops 67108864 | bytes 46137344 | tf_op jit(solution)/shard_map/vmap(jit(_solve_triangular))/triangular_solve | solution.py:20
  335.5 15.2 %fusion = bf16[2048,4096]{1,0:T(8,128)(2,1)} fusion(bf16[4,512,4096]{2,1,0:T(8,128)(2,1)} %pad_maximum_fusion, pred[2048]{0:T(1024)(128)(4,1)S(1)} %bitcast.86), kind=kLoop, calls=%fused_computation.6 | loop fusion | flops 8388608 | bytes 33556480 | tf_op jit(solution)/shard_map/convert_element_type | solution.py:24
  350.7 43.9 %fusion.14 = f32[4096,2048]{0,1:T(8,128)} fusion(bf16[2048,4096]{1,0:T(8,128)(2,1)} %fusion, s32[]{:T(128)S(6)} %select_n.36), kind=kOutput, calls=%fused_computation.23 | convolution fusion | flops 34359738368 | bytes 58720260 | tf_op jit(solution)/shard_map/dot_general | solution.py:37
  394.6 330.5 %reduce-scatter.2.cloned.1.call-done = f32[256,2048]{0,1:T(8,128)} async-done(((f32[4096,2048]{0,1:T(8,128)}), f32[256,2048]{0,1:T(8,128)}) %reduce-scatter.2.cloned.1.call-update) | async-done | bytes 2097168 | tf_op jit(solution)/shard_map/reduce_scatter | solution.py:36
  725.1 1.9 slice_select_fusion
  727.0 28.7 %all-reduce.5.cloned.1.call-done = f32[256,512]{0,1:T(8,128)} async-done(((f32[256,512]{0,1:T(8,128)}), f32[256,512]{0,1:T(8,128)}) %all-reduce.5.cloned.1.call-update) | async-done | bytes 524304 | tf_op jit(solution)/shard_map/psum | solution.py:11
  755.8 2.1 broadcast_select_fusion.1
  758.1 3.0 copy.12
  761.1 91.8 %all-reduce.7.cloned.1.call-done = (f32[256,512]{0,1:T(8,128)}, f32[256,512]{0,1:T(8,128)}) async-done(((f32[256,512]{0,1:T(8,128)}, f32[256,512]{0,1:T(8,128)}), (f32[256,512]{0,1:T(8,128)}, f32[256,512]{0,1:T(8,128)})) %all-reduce.7.cloned.1.call-update) | async-done | bytes 1048592 | tf_op jit(solution)/shard_map/psum | solution.py:11
  853.0 1.1 constant_dynamic-update-slice_fusion.1
  854.1 1.1 constant_dynamic-update-slice_fusion
  855.8 1.0 copy-done.1
  856.8 11.7 %cholesky.104 = f32[128,128]{1,0:T(8,128)S(1)} custom-call(f32[128,128]{1,0:T(8,128)S(1)} %cholesky.266), custom_call_target="Cholesky" | custom-call | tf_op jit(solution)/shard_map/jit(cholesky)/cholesky | solution.py:50
  868.7 9.8 custom-call.36
  878.5 1.2 constant_dynamic-update-slice_fusion.2
  879.7 1.3 convolution_subtract_fusion.3
  881.0 11.7 %cholesky.217 = f32[128,128]{1,0:T(8,128)S(1)} custom-call(f32[128,128]{1,0:T(8,128)S(1)} %cholesky.270), custom_call_target="Cholesky" | custom-call | tf_op jit(solution)/shard_map/jit(cholesky)/cholesky | solution.py:50
  892.8 10.0 custom-call.37
  903.0 1.3 convolution_subtract_fusion.4
  904.3 11.7 %cholesky.238 = f32[128,128]{1,0:T(8,128)S(1)} custom-call(f32[128,128]{1,0:T(8,128)S(1)} %cholesky.275), custom_call_target="Cholesky" | custom-call | tf_op jit(solution)/shard_map/jit(cholesky)/cholesky | solution.py:50
  916.7 9.8 custom-call.38
  926.8 1.2 convolution_subtract_fusion.5
  928.0 11.7 %cholesky.255 = f32[128,128]{1,0:T(8,128)S(1)} custom-call(f32[128,128]{1,0:T(8,128)S(1)} %convolution_subtract_fusion.5), custom_call_target="Cholesky" | custom-call | tf_op jit(solution)/shard_map/jit(cholesky)/cholesky | solution.py:50
  939.7 0.7 compare_reduce_fusion
  944.0 10.6 %while.3 = (s32[]{:T(128)}, f32[512,512]{1,0:T(8,128)S(1)}, s32[4,2]{0,1:T(2,128)S(1)}, f32[4,128,128]{2,1,0:T(8,128)}, s32[]{:T(128)}) while((s32[]{:T(128)}, f32[512,512]{1,0:T(8,128)S(1)}, s32[4,2]{0,1:T(2,128)S(1)}, f32[4,128,128]{2,1,0:T(8,128)}, s32[]{:T(128)}) %tuple.62), condition=%wide.while_cond.1, body=%wide.while_body.1.sunk | while | flops 2 | bytes 132705 | solution.py:51
  944.7 2.0 bitcast_dynamic-update-slice_fusion.5
  947.4 2.0 bitcast_dynamic-update-slice_fusion.5
  950.0 2.0 bitcast_dynamic-update-slice_fusion.5
  952.6 2.0 bitcast_dynamic-update-slice_fusion.5
  954.6 40.1 %custom-call.39 = f32[4,128,128]{1,2,0:T(8,128)S(1)} custom-call(f32[4,128,128]{2,1,0:T(8,128)} %get-tuple-element.17), custom_call_target="InvertDiagBlocksLowerTriangular" | custom-call | tf_op jit(solution)/shard_map/jit(_solve_triangular)/triangular_solve | solution.py:51
  997.8 2.8 fusion.28
  (63 shorter events, 12.2 us)
Async XLA Ops:
  7.2 176.4 %copy-start.4 = (s32[4]{0:T(128)S(1)}, s32[4]{0:T(128)}, u32[]{:S(2)}) copy-start(s32[4]{0:T(128)} %param.5) | copy-start | bytes 52
  7.2 204.0 %all-gather.2.cloned.1.call-start = ((), (), s32[]{:S(2)}) async-start(), calls=%async_computation.1 | async-start | bytes 25165824 | tf_op jit(solution)/shard_map/all_gather | solution.py:29
  7.9 717.2 %reduce-scatter.2.cloned.1.call-start = ((), (), s32[]{:S(2)}) async-start(), calls=%async_computation.2 | async-start | bytes 35651584 | tf_op jit(solution)/shard_map/reduce_scatter | solution.py:36
  25.8 0.6 copy-start.2
  235.6 20.4 %copy-start = (f32[4,128,4096]{2,1,0:T(8,128)}, f32[4,128,4096]{2,1,0:T(8,128)S(1)}, u32[]{:S(2)}) copy-start(f32[4,128,4096]{2,1,0:T(8,128)S(1)} %fusion.16) | copy-start | bytes 25165828
  394.5 361.2 %all-reduce.5.cloned.1.call-start = ((), (), s32[]{:S(2)}) async-start(), calls=%async_computation.3 | async-start | bytes 1048576 | tf_op jit(solution)/shard_map/psum | solution.py:11
  727.0 126.0 %all-reduce.7.cloned.1.call-start = ((), (), s32[]{:S(2)}) async-start(), calls=%async_computation.4 | async-start | bytes 2097152 | tf_op jit(solution)/shard_map/psum | solution.py:11
  758.1 185.9 %copy-start.3 = (s32[4,2]{0,1:T(2,128)S(1)}, s32[4,2]{0,1:T(2,128)}, u32[]{:S(2)}) copy-start(s32[4,2]{0,1:T(2,128)} %copy-done.2) | copy-start | bytes 100
  855.8 1.0 copy-start.1
Sparse Core Ops, SparseCore 0:
  9.5 201.5 all-gather.1
  394.7 330.3 reduce-scatter.1
  728.0 27.7 all-reduce.4
  759.1 93.7 all-reduce.6
where the time goes:
time: 1010 us
  waiting for transfers between devices  479 us (47%)
  other arithmetic  336 us (33%)
  matrix products  144 us (14%)
  local copies, waits for them, and re-layouts  30.8 us (3%)
  between operations  17.1 us (2%)
    reduce_scatter x1, waiting for transfers between devices, body(): lax.psum_scatter(lax.dot_general(gathered, own_panel, (((0,), (0,)), ((),...  330 us
    another operation x5, other arithmetic, whiten(): jax.scipy.linalg.solve_triangular(factor, right, lower=True)  179 us
    psum x2, waiting for transfers between devices, from_root(): return lax.psum(kept, axis)  121 us
    another operation x7, matrix products, whiten(): jax.scipy.linalg.solve_triangular(factor, right, lower=True)  88.9 us
    another operation x14, other arithmetic, body(): lead_factor = jnp.linalg.cholesky(leading_block)  78.7 us
    dot_general x1, matrix products, body(): lax.dot_general(gathered, own_panel, (((0,), (0,)), ((), ())), preferred_...  43.9 us
    another operation x2, other arithmetic, body(): jax.scipy.linalg.solve_triangular(lead_factor, jnp.eye(LEAD, dtype=jnp.fl...  40.2 us
    all_gather x1, waiting for transfers between devices, body(): raw_rows = lax.all_gather(blocks, 'col', axis=1, tiled=True)  27.5 us
  transfers between devices with their start and end apart: 4, of which 4 were waited for; matrix products, arithmetic and copies ran while one was open for 18% of the time, Pallas kernels for 0%

commit v1 on v0

--- a/solution.py
+++ b/solution.py
@@ -8,7 +8,7 @@
 
 def from_root(value, axis, source):
     kept = jnp.where(lax.axis_index(axis) == source, value, 0).astype(value.dtype)
-    return lax.psum(kept, axis)
+    return jnp.sum(lax.all_gather(kept, axis), axis=0)
 
 
 def whiten(segment, factors, block_live):

time: 1010 us -> 1070 us (1.059)
  waiting for transfers between devices: 479 us -> 523 us
  other arithmetic: 336 us -> 348 us
    all_gather x0 -> x3, waiting for transfers between devices: none -> 163 us  [from_root(): return jnp.sum(lax.all_gather(kept, axis), axis=0)]
    psum x2 -> x0, waiting for transfers between devices: 121 us -> none  [from_root(): return lax.psum(kept, axis)]
  transfers between devices with their start and end apart: 4 -> 5, of which waited for: 4 -> 5; matrix products, arithmetic and copies ran while one was open for 18% -> 17% of each run, Pallas kernels for 0% -> 0%
where the time goes in v1:
time: 1070 us; the launch traced here: 1060 us
  waiting for transfers between devices  523 us (49%)
  other arithmetic  348 us (33%)
  matrix products  145 us (14%)
  local copies, waits for them, and re-layouts  27.6 us (3%)
  between operations  16.9 us (2%)
    reduce_scatter x1, waiting for transfers between devices, body(): lax.psum_scatter(lax.dot_general(gathered, own_panel, (((0,), (0,)), ((),...  331 us
    another operation x5, other arithmetic, whiten(): jax.scipy.linalg.solve_triangular(factor, right, lower=True)  179 us
    all_gather x3, waiting for transfers between devices, from_root(): return jnp.sum(lax.all_gather(kept, axis), axis=0)  163 us
    another operation x7, matrix products, whiten(): jax.scipy.linalg.solve_triangular(factor, right, lower=True)  88.8 us
    another operation x14, other arithmetic, body(): lead_factor = jnp.linalg.cholesky(leading_block)  79.1 us
    dot_general x1, matrix products, body(): lax.dot_general(gathered, own_panel, (((0,), (0,)), ((), ())), preferred_...  43.9 us
    another operation x2, other arithmetic, body(): jax.scipy.linalg.solve_triangular(lead_factor, jnp.eye(LEAD, dtype=jnp.fl...  40.4 us
    all_gather x1, waiting for transfers between devices, body(): raw_rows = lax.all_gather(blocks, 'col', axis=1, tiled=True)  28.1 us
  transfers between devices with their start and end apart: 5, of which 5 were waited for; matrix products, arithmetic and copies ran while one was open for 17% of the time, Pallas kernels for 0%

profile of v1, /device:TPU:0, one launch (start us, length us, event | category | flops | bytes accessed | tf_op | source)
XLA Modules:
  0.0 1061.5 jit_solution(14004384641068398296)
XLA Ops:
  8.1 4.8 broadcast_select_fusion
  12.8 12.9 %while.2 = (s32[]{:T(128)}, f32[4,512,512]{2,1,0:T(8,128)}, s32[4,2]{0,1:T(2,128)S(1)}, f32[4,4,128,128]{3,2,0,1:T(8,128)S(1)}, s32[]{:T(128)}) while((s32[]{:T(128)}, f32[4,512,512]{2,1,0:T(8,128)}, s32[4,2]{0,1:T(2,128)S(1)}, f32[4,4,128,128]{3,2,0,1:T(8,128)S(1)}, s32[]{:T(128)}) %tuple.46), condition=%wide.while_cond, body=%wide.while_body.sunk | while | flops 2 | bytes 524397 | solution.py:20
  13.5 2.5 bitcast_dynamic-update-slice_fusion.4
  16.6 2.6 bitcast_dynamic-update-slice_fusion.4
  19.9 2.7 bitcast_dynamic-update-slice_fusion.4
  23.3 2.4 bitcast_dynamic-update-slice_fusion.4
  25.8 157.2 %custom-call.35 = f32[4,4,128,128]{2,3,1,0:T(8,128)S(1)} custom-call(f32[4,4,128,128]{3,2,1,0:T(8,128)S(1)} %bitcast.93), custom_call_target="InvertDiagBlocksLowerTriangular" | custom-call | tf_op jit(solution)/shard_map/vmap(jit(_solve_triangular))/triangular_solve | solution.py:20
  183.1 28.1 %all-gather.8.cloned.1.call-done = bf16[2048,4096]{1,0:T(8,128)(2,1)} async-done(((bf16[2048,2048]{1,0:T(8,128)(2,1)}), bf16[2048,4096]{1,0:T(8,128)(2,1)}) %all-gather.8.cloned.1.call-update) | async-done | bytes 16777232 | tf_op jit(solution)/shard_map/all_gather | solution.py:29
  211.2 18.6 %convert_element_type.17 = f32[4,512,4096]{2,1,0:T(8,128)} convert(bf16[4,512,4096]{2,1,0:T(8,128)(2,1)} %bitcast.87) | non-fusion elementwise | flops 8388608 | bytes 50331648 | tf_op jit(solution)/shard_map/convert_element_type | solution.py:18
  229.8 5.5 fusion.16
  235.3 8.8 fusion.36
  244.1 11.6 %fusion.13 = f32[4,128,4096]{2,1,0:T(8,128)} fusion(f32[4,128,4096]{2,1,0:T(8,128)S(1)} %fusion.36, f32[4,512,4096]{2,1,0:T(8,128)} %convert_element_type.17, f32[4,4,128,128]{2,3,1,0:T(8,128)S(1)} %custom-call.35), kind=kOutput, calls=%fused_computation.22 | convolution fusion | flops 3223322624 | bytes 25427968 | tf_op jit(solution)/shard_map/vmap(jit(_solve_triangular))/triangular_solve | solution.py:20
  255.7 14.2 %fusion.7 = f32[4,128,4096]{2,1,0:T(8,128)} fusion(f32[4,128,4096]{2,1,0:T(8,128)} %fusion.13, f32[4,128,4096]{2,1,0:T(8,128)S(1)} %fusion.16, f32[4,512,512]{2,1,0:T(8,128)} %get-tuple-element.150), kind=kOutput, calls=%fused_computation.13 | convolution fusion | flops 6446645248 | bytes 25690112 | tf_op jit(solution)/shard_map/vmap(jit(_solve_triangular))/triangular_solve | solution.py:20
  269.9 12.9 %fusion.12 = f32[4,128,4096]{2,1,0:T(8,128)} fusion(f32[4,128,4096]{2,1,0:T(8,128)} %fusion.7, f32[4,512,4096]{2,1,0:T(8,128)} %convert_element_type.17, f32[4,4,128,128]{2,3,1,0:T(8,128)S(1)} %custom-call.35), kind=kOutput, calls=%fused_computation.20 | convolution fusion | flops 3223322624 | bytes 25427968 | tf_op jit(solution)/shard_map/vmap(jit(_solve_triangular))/triangular_solve | solution.py:20
  282.8 23.3 %fusion.1 = f32[4,128,4096]{2,1,0:T(8,128)} fusion(f32[4,128,4096]{2,1,0:T(8,128)} %fusion.12, f32[4,128,4096]{2,1,0:T(8,128)} %fusion.13, f32[4,128,4096]{2,1,0:T(8,128)} %copy-done, f32[4,512,512]{2,1,0:T(8,128)} %get-tuple-element.150), kind=kOutput, calls=%fused_computation.7 | convolution fusion | flops 9676259328 | bytes 34340864 | tf_op jit(solution)/shard_map/vmap(jit(_solve_triangular))/triangular_solve | solution.py:20
  306.1 12.5 %fusion.11 = bf16[4,128,4096]{2,1,0:T(8,128)(2,1)} fusion(f32[4,128,4096]{2,1,0:T(8,128)} %fusion.1, f32[4,512,4096]{2,1,0:T(8,128)} %convert_element_type.17, f32[4,4,128,128]{2,3,1,0:T(8,128)S(1)} %custom-call.35), kind=kOutput, calls=%fused_computation.18 | convolution fusion | flops 3223322624 | bytes 21233664 | tf_op jit(solution)/shard_map/vmap(jit(_solve_triangular))/triangular_solve | solution.py:20
  318.6 16.8 %pad_maximum_fusion = bf16[4,512,4096]{2,1,0:T(8,128)(2,1)} fusion(bf16[4,128,4096]{2,1,0:T(8,128)(2,1)} %fusion.11, f32[4,128,4096]{2,1,0:T(8,128)} %fusion.12, f32[4,128,4096]{2,1,0:T(8,128)} %fusion.13, f32[4,128,4096]{2,1,0:T(8,128)} %copy-done), kind=kLoop, calls=%fused_computation.4 | loop fusion | flops 67108864 | bytes 46137344 | tf_op jit(solution)/shard_map/vmap(jit(_solve_triangular))/triangular_solve | solution.py:20
  335.4 15.2 %fusion = bf16[2048,4096]{1,0:T(8,128)(2,1)} fusion(bf16[4,512,4096]{2,1,0:T(8,128)(2,1)} %pad_maximum_fusion, pred[2048]{0:T(1024)(128)(4,1)S(1)} %bitcast.92), kind=kLoop, calls=%fused_computation.6 | loop fusion | flops 8388608 | bytes 33556480 | tf_op jit(solution)/shard_map/convert_element_type | solution.py:24
  350.6 43.9 %fusion.14 = f32[4096,2048]{1,0:T(8,128)} fusion(bf16[2048,4096]{1,0:T(8,128)(2,1)} %fusion, s32[]{:T(128)S(6)} %select_n.56), kind=kOutput, calls=%fused_computation.23 | convolution fusion | flops 34359738368 | bytes 58720260 | tf_op jit(solution)/shard_map/dot_general | solution.py:37
  394.5 330.6 %reduce-scatter.2.cloned.1.call-done = f32[256,2048]{1,0:T(8,128)} async-done(((f32[4096,2048]{1,0:T(8,128)}), f32[256,2048]{1,0:T(8,128)}) %reduce-scatter.2.cloned.1.call-update) | async-done | bytes 2097168 | tf_op jit(solution)/shard_map/reduce_scatter | solution.py:36
  725.2 1.9 slice_select_fusion
  727.2 20.5 %all-gather.10.cloned.1.call-done = f32[512,512]{1,0:T(8,128)} async-done(((f32[256,512]{1,0:T(8,128)}), f32[512,512]{1,0:T(8,128)}) %all-gather.10.cloned.1.call-update) | async-done | bytes 1048592 | tf_op jit(solution)/shard_map/all_gather | solution.py:11
  747.6 1.4 reduce_sum.27
  752.0 72.7 %all-gather.12.cloned.1.call-done = f32[4096,512]{1,0:T(8,128)} async-done(((f32[256,512]{1,0:T(8,128)}), f32[4096,512]{1,0:T(8,128)}) %all-gather.12.cloned.1.call-update) | async-done | bytes 8388624 | tf_op jit(solution)/shard_map/all_gather | solution.py:11
  824.6 4.4 reduce_sum.28
  829.2 70.3 %all-gather.14.cloned.1.call-done = f32[4096,512]{1,0:T(8,128)} async-done(((f32[256,512]{1,0:T(8,128)}), f32[4096,512]{1,0:T(8,128)}) %all-gather.14.cloned.1.call-update) | async-done | bytes 8388624 | tf_op jit(solution)/shard_map/all_gather | solution.py:11
  899.6 4.4 reduce_sum.29
  905.3 1.6 copy.18
  908.0 11.7 %cholesky.104 = f32[128,128]{1,0:T(8,128)S(1)} custom-call(f32[128,128]{1,0:T(8,128)S(1)} %cholesky.266), custom_call_target="Cholesky" | custom-call | tf_op jit(solution)/shard_map/jit(cholesky)/cholesky | solution.py:50
  919.9 9.8 custom-call.36
  929.7 1.2 constant_dynamic-update-slice_fusion
  931.0 1.3 convolution_subtract_fusion.3
  932.3 12.1 %cholesky.217 = f32[128,128]{1,0:T(8,128)S(1)} custom-call(f32[128,128]{1,0:T(8,128)S(1)} %cholesky.270), custom_call_target="Cholesky" | custom-call | tf_op jit(solution)/shard_map/jit(cholesky)/cholesky | solution.py:50
  944.4 9.8 custom-call.37
  954.5 1.3 convolution_subtract_fusion.4
  955.8 11.7 %cholesky.238 = f32[128,128]{1,0:T(8,128)S(1)} custom-call(f32[128,128]{1,0:T(8,128)S(1)} %cholesky.275), custom_call_target="Cholesky" | custom-call | tf_op jit(solution)/shard_map/jit(cholesky)/cholesky | solution.py:50
  968.3 9.8 custom-call.38
  978.3 1.2 convolution_subtract_fusion.5
  979.5 11.9 %cholesky.255 = f32[128,128]{1,0:T(8,128)S(1)} custom-call(f32[128,128]{1,0:T(8,128)S(1)} %convolution_subtract_fusion.5), custom_call_target="Cholesky" | custom-call | tf_op jit(solution)/shard_map/jit(cholesky)/cholesky | solution.py:50
  996.5 11.7 %while.3 = (s32[]{:T(128)}, f32[512,512]{1,0:T(8,128)}, s32[4,2]{0,1:T(2,128)S(1)}, f32[4,128,128]{2,1,0:T(8,128)S(1)}, s32[]{:T(128)}) while((s32[]{:T(128)}, f32[512,512]{1,0:T(8,128)}, s32[4,2]{0,1:T(2,128)S(1)}, f32[4,128,128]{2,1,0:T(8,128)S(1)}, s32[]{:T(128)}) %tuple.62), condition=%wide.while_cond.1, body=%wide.while_body.1.sunk | while | flops 2 | bytes 131181 | solution.py:51
  997.2 2.3 bitcast_dynamic-update-slice_fusion.5
  1000.1 2.3 bitcast_dynamic-update-slice_fusion.5
  1003.1 2.3 bitcast_dynamic-update-slice_fusion.5
  1006.0 2.2 bitcast_dynamic-update-slice_fusion.5
  1008.2 39.3 %custom-call.39 = f32[4,128,128]{1,2,0:T(8,128)S(1)} custom-call(f32[4,128,128]{2,1,0:T(8,128)S(1)} %get-tuple-element.17), custom_call_target="InvertDiagBlocksLowerTriangular" | custom-call | tf_op jit(solution)/shard_map/jit(_solve_triangular)/triangular_solve | solution.py:51
  1049.5 1.3 convolution_subtract_fusion
  1051.3 1.6 convolution_subtract_fusion.2
  1053.3 1.5 fusion.28
  (67 shorter events, 18.8 us)
Async XLA Ops:
  7.2 175.8 %copy-start.3 = (s32[4]{0:T(128)S(1)}, s32[4]{0:T(128)}, u32[]{:S(2)}) copy-start(s32[4]{0:T(128)} %param.5) | copy-start | bytes 52
  7.2 204.0 %all-gather.8.cloned.1.call-start = ((), (), s32[]{:S(2)}) async-start(), calls=%async_computation.1 | async-start | bytes 25165824 | tf_op jit(solution)/shard_map/all_gather | solution.py:29
  7.9 717.3 %reduce-scatter.2.cloned.1.call-start = ((), (), s32[]{:S(2)}) async-start(), calls=%async_computation.2 | async-start | bytes 35651584 | tf_op jit(solution)/shard_map/reduce_scatter | solution.py:36
  235.3 20.4 %copy-start = (f32[4,128,4096]{2,1,0:T(8,128)}, f32[4,128,4096]{2,1,0:T(8,128)S(1)}, u32[]{:S(2)}) copy-start(f32[4,128,4096]{2,1,0:T(8,128)S(1)} %fusion.16) | copy-start | bytes 25165828
  394.5 353.1 %all-gather.10.cloned.1.call-start = ((), (), s32[]{:S(2)}) async-start(), calls=%async_computation.3 | async-start | bytes 1572864 | tf_op jit(solution)/shard_map/all_gather | solution.py:11
  727.1 97.5 %all-gather.12.cloned.1.call-start = ((), (), s32[]{:S(2)}) async-start(), calls=%async_computation.4 | async-start | bytes 8912896 | tf_op jit(solution)/shard_map/all_gather | solution.py:11
  750.2 149.4 %all-gather.14.cloned.1.call-start = ((), (), s32[]{:S(2)}) async-start(), calls=%async_computation.5 | async-start | bytes 8912896 | tf_op jit(solution)/shard_map/all_gather | solution.py:11
  907.0 1.0 copy-start.2
  908.0 139.8 %copy-start.1 = (f32[512,512]{1,0:T(8,128)S(1)}, f32[512,512]{1,0:T(8,128)}, u32[]{:S(2)}) copy-start(f32[512,512]{1,0:T(8,128)} %fusion.34) | copy-start | bytes 3145732
Sparse Core Ops, SparseCore 0:
  9.5 201.5 all-gather.7
  394.6 330.5 reduce-scatter.1
  727.2 20.3 all-gather.9
  750.3 74.2 all-gather.11
  826.6 72.8 all-gather.13
